TPU v7x, 512 devices: a whole 4x4x16 slice. The times are simulated.
512 devices in a mesh: wide: 128 (over y_hi, x, z), narrow: 4 (over y_lo, core).
Axes of the slice: x: 4, y: 4 (y_hi: 2, y_lo: 2; y = y_hi * 2 + y_lo), z: 16, core: 2. Of those that a mesh axis runs over, the one named last changes fastest.
Arguments:
- treated: bfloat16 [131072, 512], P(('wide', 'narrow')), may hold values from -6 to 6
- control: bfloat16 [131072, 512], P('wide'), may hold values from -6 to 6
- treated_weight: float32 [131072], P(('wide', 'narrow')), may hold values from 0.5 to 2
- control_weight: float32 [131072], replicated, may hold values from 0.5 to 2
- band: int32 [1024, 24], P(('wide', 'narrow')), may hold values from 0 to 1, as said below
Outputs:
- grad_treated: float32 [131072, 512], P(('wide', 'narrow'))
- grad_control: float32 [131072, 512], P(('wide', 'narrow'))
Inputs may be any that keep to these rules, and one draw needn't show every extreme that they name: band[t, k] = 1 pairs treated block t with control block (t // 8 - 1) * 8 + k. For each t the ones form one run of k that contains k = 8 + t % 8; every k whose control block lies outside 0 to 1023 is 0.
All inputs are finite; a program needn't handle non-finite values.
Results may differ from a plain program's by a relative error of at most 0.0055.
Values may be sent and summed in bfloat16 or wider, within the bound.
No kernel may reach another device: no remote copies, remote signals or barrier semaphores. Data moves between devices by JAX's collectives and lax.ppermute only.
A program may use at most 64 MiB of HBM per device.

v0:
```python
import jax
import jax.numpy as jnp
from jax import lax
from jax.sharding import PartitionSpec as P

SWEEPS = 2
SMOOTHING_TEMP = 0.05
EPSILON = 1e-06


def extended(block, sides, width):
    for axis, dim in sides:
        count = lax.axis_size(axis)
        forward = [(i, i + 1) for i in range(count - 1)]
        backward = [(target, source) for source, target in forward]
        low = lax.ppermute(
            lax.slice_in_dim(block, block.shape[dim] - width, None, axis=dim), axis, forward
        )
        high = lax.ppermute(lax.slice_in_dim(block, 0, width, axis=dim), axis, backward)
        block = jnp.concatenate([low, block, high], axis=dim)
    return block


def normalize(features):
    values = features.astype(jnp.float32)
    return (values * lax.rsqrt(jnp.mean(values * values, axis=1, keepdims=True) + EPSILON)).astype(
        jnp.bfloat16
    )


def expand(pair_blocks, block_rows):
    block_count, column_count = pair_blocks.shape
    full = jnp.broadcast_to(
        pair_blocks[:, None, :, None], (block_count, block_rows, column_count, block_rows)
    )
    return full.reshape(block_count * block_rows, column_count * block_rows)


def shards(treated, control, treated_weight, control_weight, band):
    row_count = treated.shape[0]
    slab_rows = control.shape[0]
    feature_total = treated.shape[1]
    block_rows = row_count // band.shape[0]
    wide_index = lax.axis_index("wide")
    narrow_index = lax.axis_index("narrow")
    treated_norm = normalize(treated)
    own_slab = normalize(control)
    band_span = extended(own_slab[None], (("wide", 0),), 1)
    band_span = band_span.reshape(3 * slab_rows, feature_total)
    paired_mask = expand(band, block_rows) > 0
    scale_factor = 1.0 / (feature_total * SMOOTHING_TEMP)
    pairwise_inner = lax.dot_general(
        treated_norm, band_span, (((1,), (1,)), ((), ())), preferred_element_type=jnp.float32
    )
    kernel = jnp.where(paired_mask, jnp.exp(pairwise_inner * scale_factor), 0.0)
    scales = jnp.ones((3 * slab_rows,), jnp.float32)
    own_weight_slab = lax.dynamic_slice_in_dim(control_weight, wide_index * slab_rows, slab_rows)
    row_scale = treated_weight
    for sweep_index in range(SWEEPS):
        row_scale = treated_weight / jnp.sum(kernel * scales[None, :], axis=1)
        column_parts = jnp.sum(kernel * row_scale[:, None], axis=0).reshape(3, slab_rows)
        slab_parts = lax.psum(column_parts, "narrow")
        edges = extended(slab_parts[None], (("wide", 0),), 1)
        column_total = edges[1, 1] + edges[0, 2] + edges[2, 0]
        col_scale = own_weight_slab / column_total
        scales = extended(col_scale[None], (("wide", 0),), 1).reshape(3 * slab_rows)
    transport = row_scale[:, None] * kernel * scales[None, :]
    plan_bf = transport.astype(jnp.bfloat16)
    pulled = jnp.dot(plan_bf, band_span, preferred_element_type=jnp.float32)
    grad_treated = jnp.sum(transport, axis=1)[:, None] * treated_norm.astype(jnp.float32) - pulled
    quarter = slab_rows // lax.axis_size("narrow")
    pushed = lax.dot_general(
        plan_bf, treated_norm, (((0,), (0,)), ((), ())), preferred_element_type=jnp.float32
    )
    pushed = pushed.reshape(3, slab_rows, feature_total)
    neighbours = extended(pushed, (("wide", 0),), 1)
    summed = lax.psum_scatter(
        neighbours[0] + neighbours[2] + neighbours[4], "narrow", scatter_dimension=0, tiled=True
    )
    own_rows = lax.dynamic_slice_in_dim(own_slab, narrow_index * quarter, quarter, 0).astype(
        jnp.float32
    )
    own_weight = lax.dynamic_slice_in_dim(
        control_weight, wide_index * slab_rows + narrow_index * quarter, quarter
    )
    grad_control = own_weight[:, None] * own_rows - summed
    return (grad_treated, grad_control)


def solution(mesh):
    return jax.shard_map(
        shards,
        mesh=mesh,
        in_specs=(
            P(("wide", "narrow"), None),
            P("wide", None),
            P(("wide", "narrow")),
            P(),
            P(("wide", "narrow"), None),
        ),
        out_specs=(P(("wide", "narrow"), None), P(("wide", "narrow"), None)),
        check_vma=False,
    )
```

profile of v0, /device:TPU:1, one launch (start us, length us, event | category | flops | bytes accessed | tf_op | source)
XLA Modules:
  0.0 227.1 jit_solution(4623724721699542760)
XLA Ops:
  7.2 0.0 reduce-scatter.2.cloned.1.call-start
  7.2 1.5 fusion.2
  8.8 1.5 fusion.13
  10.3 1.3 collective-permute-start.1
  11.6 5.1 %collective-permute-start = (bf16[1,1024,512]{2,1,0:T(8,128)(2,1)S(1)}, bf16[1,1024,512]{2,1,0:T(8,128)(2,1)S(1)}, u32[]{:S(2)}, u32[]{:S(2)}) collective-permute-start(bf16[1,1024,512]{2,1,0:T(8,128)(2,1)S(1)} %fusion.13), channel_id=1, source_target_pairs={{0,4},{4,8},{8,12},{12,16},{16,20},{20,24},{24,28},{28,32},{32,36}... | collective-permute-start | bytes 3145736 | tf_op jit(solution)/shard_map/ppermute | solution.py:16
  16.7 0.1 fusion.5
  16.8 15.2 %collective-permute-done.1 = bf16[1,1024,512]{2,1,0:T(8,128)(2,1)S(1)} collective-permute-done((bf16[1,1024,512]{2,1,0:T(8,128)(2,1)S(1)}, bf16[1,1024,512]{2,1,0:T(8,128)(2,1)S(1)}, u32[]{:S(2)}, u32[]{:S(2)}) %collective-permute-start.1) | collective-permute-done | bytes 1048608 | tf_op jit(solution)/shard_map/ppermute | solution.py:19
  32.1 0.9 collective-permute-done
  33.0 0.3 pad_maximum_fusion
  33.3 0.3 broadcast_in_dim.16
  33.6 0.0 copy-start.3
  33.6 1.3 fusion.10
  35.0 0.0 copy-done
  35.0 0.4 multiply_reduce_fusion.1
  35.4 25.4 %psum.14 = f32[1,3,1024]{2,1,0:T(4,128)S(1)} all-reduce(f32[1,3,1024]{2,1,0:T(4,128)S(1)} %broadcast_in_dim.35), channel_id=1, replica_groups=mesh['wide'=128,'narrow'=4] {'narrow'}, use_global_device_ids=true, to_apply=%region_4.5 | all-reduce | flops 3072 | bytes 24576 | tf_op jit(solution)/shard_map/psum | solution.py:62
  60.9 1.3 collective-permute-start.3
  62.2 4.0 %collective-permute-start.2 = (f32[1,3,1024]{2,1,0:T(4,128)S(1)}, f32[1,3,1024]{2,1,0:T(4,128)S(1)}, u32[]{:S(2)}, u32[]{:S(2)}) collective-permute-start(f32[1,3,1024]{2,1,0:T(4,128)S(1)} %psum.14), channel_id=1, source_target_pairs={{0,4},{4,8},{8,12},{12,16},{16,20},{20,24},{24,28},{28,32},{32,36}... | collective-permute-start | bytes 36872 | tf_op jit(solution)/shard_map/ppermute | solution.py:16
  66.2 0.0 collective-permute-done.3
  66.2 0.8 collective-permute-done.2
  67.0 0.7 dynamic-slice_divide_fusion.1
  67.7 1.3 collective-permute-start.5
  69.0 4.3 %collective-permute-start.4 = (f32[1,1024]{1,0:T(1,128)S(1)}, f32[1,1024]{1,0:T(1,128)S(1)}, u32[]{:S(2)}, u32[]{:S(2)}) collective-permute-start(f32[1,1024]{1,0:T(1,128)S(1)} %bitcast.28), channel_id=1, source_target_pairs={{0,4},{4,8},{8,12},{12,16},{16,20},{20,24},{24,28},{28,32},{32,36}... | collective-permute-start | bytes 12296 | tf_op jit(solution)/shard_map/ppermute | solution.py:16
  73.3 0.0 collective-permute-done.5
  73.3 0.7 collective-permute-done.4
  74.0 0.3 multiply_reduce_fusion
  74.4 0.4 multiply_reduce_fusion.3
  74.8 12.4 %psum.15 = f32[1,3,1024]{2,1,0:T(4,128)S(1)} all-reduce(f32[1,3,1024]{2,1,0:T(4,128)S(1)} %broadcast_in_dim.37), channel_id=1, replica_groups=mesh['wide'=128,'narrow'=4] {'narrow'}, use_global_device_ids=true, to_apply=%region_7.8 | all-reduce | flops 3072 | bytes 24576 | tf_op jit(solution)/shard_map/psum | solution.py:62
  87.2 1.3 collective-permute-start.7
  88.5 4.5 %collective-permute-start.6 = (f32[1,3,1024]{2,1,0:T(4,128)S(1)}, f32[1,3,1024]{2,1,0:T(4,128)S(1)}, u32[]{:S(2)}, u32[]{:S(2)}) collective-permute-start(f32[1,3,1024]{2,1,0:T(4,128)S(1)} %psum.15), channel_id=1, source_target_pairs={{0,4},{4,8},{8,12},{12,16},{16,20},{20,24},{24,28},{28,32},{32,36}... | collective-permute-start | bytes 36872 | tf_op jit(solution)/shard_map/ppermute | solution.py:16
  93.1 0.8 collective-permute-done.6
  93.9 0.7 dynamic-slice_divide_fusion
  94.6 1.3 collective-permute-start.9
  95.9 4.3 %collective-permute-start.8 = (f32[1,1024]{1,0:T(1,128)S(1)}, f32[1,1024]{1,0:T(1,128)S(1)}, u32[]{:S(2)}, u32[]{:S(2)}) collective-permute-start(f32[1,1024]{1,0:T(1,128)S(1)} %bitcast.25), channel_id=1, source_target_pairs={{0,4},{4,8},{8,12},{12,16},{16,20},{20,24},{24,28},{28,32},{32,36}... | collective-permute-start | bytes 12296 | tf_op jit(solution)/shard_map/ppermute | solution.py:16
  100.2 0.7 collective-permute-done.8
  101.0 1.1 fusion.7
  102.1 0.4 slice_bitcast_fusion.1
  102.6 1.3 collective-permute-start.11
  103.9 4.4 %collective-permute-start.10 = (f32[1,1024,512]{2,1,0:T(8,128)S(1)}, f32[1,1024,512]{2,1,0:T(8,128)S(1)}, u32[]{:S(2)}, u32[]{:S(2)}) collective-permute-start(f32[1,1024,512]{2,1,0:T(8,128)S(1)} %get-tuple-element.2), channel_id=1, source_target_pairs={{0,4},{4,8},{8,12},{12,16},{16,20},{20,24},{24,28},{28,32},{32,36}... | collective-permute-start | bytes 6291464 | tf_op jit(solution)/shard_map/ppermute | solution.py:16
  108.3 39.4 %collective-permute-done.11 = f32[1,1024,512]{2,1,0:T(8,128)S(1)} collective-permute-done((f32[1,1024,512]{2,1,0:T(8,128)S(1)}, f32[1,1024,512]{2,1,0:T(8,128)S(1)}, u32[]{:S(2)}, u32[]{:S(2)}) %collective-permute-start.11) | collective-permute-done | bytes 2097184 | tf_op jit(solution)/shard_map/ppermute | solution.py:19
  147.7 0.9 collective-permute-done.10
  148.6 2.1 fusion.4
  150.7 0.0 reduce-scatter.2.cloned.1.call-update
  150.7 0.8 dynamic_slice.10
  151.5 2.7 %fusion.3 = bf16[1024,512]{1,0:T(8,128)(2,1)} fusion(bf16[1024,512]{1,0:T(8,128)(2,1)} %param.6, f32[1024]{0:T(1024)S(1)} %add_rsqrt_fusion), kind=kLoop, calls=%fused_computation.12 | loop fusion | flops 1572864 | bytes 2101248 | tf_op jit(solution)/shard_map/convert_element_type | solution.py:26
  154.2 0.5 multiply_reduce_fusion.2
  154.7 1.8 convolution_subtract_fusion
  156.5 61.8 %reduce-scatter.2.cloned.1.call-done = f32[256,512]{1,0:T(8,128)} async-done(((f32[1024,512]{1,0:T(8,128)}), f32[256,512]{1,0:T(8,128)}) %reduce-scatter.2.cloned.1.call-update) | async-done | bytes 524304 | tf_op jit(solution)/shard_map/reduce_scatter | solution.py:77
  218.3 2.0 multiply_subtract_fusion
  (23 shorter events, 0.2 us)
Async XLA Ops:
  7.2 9.5 %copy-start.2 = (bf16[256,512]{1,0:T(8,128)(2,1)S(1)}, bf16[256,512]{1,0:T(8,128)(2,1)}, u32[]{:S(2)}) copy-start(bf16[256,512]{1,0:T(8,128)(2,1)} %param.5) | copy-start | bytes 786436
  7.2 9.6 %copy-start.4 = (s32[2,24]{1,0:T(2,128)S(1)}, s32[2,24]{1,0:T(2,128)}, u32[]{:S(2)}) copy-start(s32[2,24]{1,0:T(2,128)} %param.9) | copy-start | bytes 580
  7.2 211.1 %reduce-scatter.2.cloned.1.call-start = ((), (), s32[]{:S(2)}) async-start(), calls=%async_computation.1 | async-start | bytes 2621440 | tf_op jit(solution)/shard_map/reduce_scatter | solution.py:77
  10.3 21.8 %collective-permute-start.1 = (bf16[1,1024,512]{2,1,0:T(8,128)(2,1)S(1)}, bf16[1,1024,512]{2,1,0:T(8,128)(2,1)S(1)}, u32[]{:S(2)}, u32[]{:S(2)}) collective-permute-start(bf16[1,1024,512]{2,1,0:T(8,128)(2,1)S(1)} %fusion.13), channel_id=1, source_target_pairs={{4,0},{8,4},{12,8},{16,12},{20,16},{24,20},{28,24},{32,28},{36,32}... | collective-permute-start | bytes 3145736 | tf_op jit(solution)/shard_map/ppermute | solution.py:19
  11.6 21.4 %collective-permute-start = (bf16[1,1024,512]{2,1,0:T(8,128)(2,1)S(1)}, bf16[1,1024,512]{2,1,0:T(8,128)(2,1)S(1)}, u32[]{:S(2)}, u32[]{:S(2)}) collective-permute-start(bf16[1,1024,512]{2,1,0:T(8,128)(2,1)S(1)} %fusion.13), channel_id=1, source_target_pairs={{0,4},{4,8},{8,12},{12,16},{16,20},{20,24},{24,28},{28,32},{32,36}... | collective-permute-start | bytes 3145736 | tf_op jit(solution)/shard_map/ppermute | solution.py:16
  33.3 1.7 copy-start
  33.6 1.4 copy-start.3
  60.9 5.3 %collective-permute-start.3 = (f32[1,3,1024]{2,1,0:T(4,128)S(1)}, f32[1,3,1024]{2,1,0:T(4,128)S(1)}, u32[]{:S(2)}, u32[]{:S(2)}) collective-permute-start(f32[1,3,1024]{2,1,0:T(4,128)S(1)} %psum.14), channel_id=1, source_target_pairs={{4,0},{8,4},{12,8},{16,12},{20,16},{24,20},{28,24},{32,28},{36,32}... | collective-permute-start | bytes 36872 | tf_op jit(solution)/shard_map/ppermute | solution.py:19
  62.2 4.8 %collective-permute-start.2 = (f32[1,3,1024]{2,1,0:T(4,128)S(1)}, f32[1,3,1024]{2,1,0:T(4,128)S(1)}, u32[]{:S(2)}, u32[]{:S(2)}) collective-permute-start(f32[1,3,1024]{2,1,0:T(4,128)S(1)} %psum.14), channel_id=1, source_target_pairs={{0,4},{4,8},{8,12},{12,16},{16,20},{20,24},{24,28},{28,32},{32,36}... | collective-permute-start | bytes 36872 | tf_op jit(solution)/shard_map/ppermute | solution.py:16
  67.7 5.6 %collective-permute-start.5 = (f32[1,1024]{1,0:T(1,128)S(1)}, f32[1,1024]{1,0:T(1,128)S(1)}, u32[]{:S(2)}, u32[]{:S(2)}) collective-permute-start(f32[1,1024]{1,0:T(1,128)S(1)} %bitcast.27), channel_id=1, source_target_pairs={{4,0},{8,4},{12,8},{16,12},{20,16},{24,20},{28,24},{32,28},{36,32}... | collective-permute-start | bytes 12296 | tf_op jit(solution)/shard_map/ppermute | solution.py:19
  69.0 5.0 %collective-permute-start.4 = (f32[1,1024]{1,0:T(1,128)S(1)}, f32[1,1024]{1,0:T(1,128)S(1)}, u32[]{:S(2)}, u32[]{:S(2)}) collective-permute-start(f32[1,1024]{1,0:T(1,128)S(1)} %bitcast.28), channel_id=1, source_target_pairs={{0,4},{4,8},{8,12},{12,16},{16,20},{20,24},{24,28},{28,32},{32,36}... | collective-permute-start | bytes 12296 | tf_op jit(solution)/shard_map/ppermute | solution.py:16
  87.2 5.8 %collective-permute-start.7 = (f32[1,3,1024]{2,1,0:T(4,128)S(1)}, f32[1,3,1024]{2,1,0:T(4,128)S(1)}, u32[]{:S(2)}, u32[]{:S(2)}) collective-permute-start(f32[1,3,1024]{2,1,0:T(4,128)S(1)} %psum.15), channel_id=1, source_target_pairs={{4,0},{8,4},{12,8},{16,12},{20,16},{24,20},{28,24},{32,28},{36,32}... | collective-permute-start | bytes 36872 | tf_op jit(solution)/shard_map/ppermute | solution.py:19
  88.5 5.4 %collective-permute-start.6 = (f32[1,3,1024]{2,1,0:T(4,128)S(1)}, f32[1,3,1024]{2,1,0:T(4,128)S(1)}, u32[]{:S(2)}, u32[]{:S(2)}) collective-permute-start(f32[1,3,1024]{2,1,0:T(4,128)S(1)} %psum.15), channel_id=1, source_target_pairs={{0,4},{4,8},{8,12},{12,16},{16,20},{20,24},{24,28},{28,32},{32,36}... | collective-permute-start | bytes 36872 | tf_op jit(solution)/shard_map/ppermute | solution.py:16
  94.6 5.6 %collective-permute-start.9 = (f32[1,1024]{1,0:T(1,128)S(1)}, f32[1,1024]{1,0:T(1,128)S(1)}, u32[]{:S(2)}, u32[]{:S(2)}) collective-permute-start(f32[1,1024]{1,0:T(1,128)S(1)} %bitcast.24), channel_id=1, source_target_pairs={{4,0},{8,4},{12,8},{16,12},{20,16},{24,20},{28,24},{32,28},{36,32}... | collective-permute-start | bytes 12296 | tf_op jit(solution)/shard_map/ppermute | solution.py:19
  95.9 5.0 %collective-permute-start.8 = (f32[1,1024]{1,0:T(1,128)S(1)}, f32[1,1024]{1,0:T(1,128)S(1)}, u32[]{:S(2)}, u32[]{:S(2)}) collective-permute-start(f32[1,1024]{1,0:T(1,128)S(1)} %bitcast.25), channel_id=1, source_target_pairs={{0,4},{4,8},{8,12},{12,16},{16,20},{20,24},{24,28},{28,32},{32,36}... | collective-permute-start | bytes 12296 | tf_op jit(solution)/shard_map/ppermute | solution.py:16
  102.6 45.1 %collective-permute-start.11 = (f32[1,1024,512]{2,1,0:T(8,128)S(1)}, f32[1,1024,512]{2,1,0:T(8,128)S(1)}, u32[]{:S(2)}, u32[]{:S(2)}) collective-permute-start(f32[1,1024,512]{2,1,0:T(8,128)S(1)} %get-tuple-element.3), channel_id=1, source_target_pairs={{4,0},{8,4},{12,8},{16,12},{20,16},{24,20},{28,24},{32,28},{36,32}... | collective-permute-start | bytes 6291464 | tf_op jit(solution)/shard_map/ppermute | solution.py:19
  103.9 44.7 %collective-permute-start.10 = (f32[1,1024,512]{2,1,0:T(8,128)S(1)}, f32[1,1024,512]{2,1,0:T(8,128)S(1)}, u32[]{:S(2)}, u32[]{:S(2)}) collective-permute-start(f32[1,1024,512]{2,1,0:T(8,128)S(1)} %get-tuple-element.2), channel_id=1, source_target_pairs={{0,4},{4,8},{8,12},{12,16},{16,20},{20,24},{24,28},{28,32},{32,36}... | collective-permute-start | bytes 6291464 | tf_op jit(solution)/shard_map/ppermute | solution.py:16
  151.5 3.2 %copy-start.1 = (bf16[3,1024,512]{2,1,0:T(8,128)(2,1)S(1)}, bf16[3,1024,512]{2,1,0:T(8,128)(2,1)}, u32[]{:S(2)}) copy-start(bf16[3,1024,512]{2,1,0:T(8,128)(2,1)} %copy-done) | copy-start | bytes 9437188
Sparse Core Ops, SparseCore 0:
  150.8 67.3 reduce-scatter.1
where the time goes:
time: 228 us; the launch traced here: 227 us
  waiting for transfers between devices  121 us (53%)
  blocking collectives  37.8 us (17%)
  starting transfers between devices  34.2 us (15%)
  between operations  14.3 us (6%)
  other arithmetic  13.5 us (6%)
  matrix products  4.31 us (2%)
    reduce_scatter x1, waiting for transfers between devices, shards(): lax.psum_scatter(neighbours[0] + neighbours[2] + neighbours[4], 'narrow',...  61.8 us
    ppermute x6, waiting for transfers between devices, extended(): lax.ppermute(lax.slice_in_dim(block, 0, width, axis=dim), axis, backward)  54.7 us
    psum x2, blocking collectives, shards(): slab_parts = lax.psum(column_parts, 'narrow')  37.8 us
    ppermute x6, starting transfers between devices, extended(): lax.ppermute(lax.slice_in_dim(block, block.shape[dim] - width, None, axis...  26.5 us
    ppermute x6, starting transfers between devices, extended(): lax.ppermute(lax.slice_in_dim(block, 0, width, axis=dim), axis, backward)  7.71 us
    ppermute x6, waiting for transfers between devices, extended(): lax.ppermute(lax.slice_in_dim(block, block.shape[dim] - width, None, axis...  4.93 us
  transfers between devices with their start and end apart: 13, of which 9 were waited for; matrix products, arithmetic and copies ran while one was open for 3% of the time, Pallas kernels for 0%

commit v1 on v0

--- a/solution.py
+++ b/solution.py
@@ -59,7 +59,7 @@
     for sweep_index in range(SWEEPS):
         row_scale = treated_weight / jnp.sum(kernel * scales[None, :], axis=1)
         column_parts = jnp.sum(kernel * row_scale[:, None], axis=0).reshape(3, slab_rows)
-        slab_parts = lax.psum(column_parts, "narrow")
+        slab_parts = jnp.sum(lax.all_gather(column_parts, "narrow"), axis=0)
         edges = extended(slab_parts[None], (("wide", 0),), 1)
         column_total = edges[1, 1] + edges[0, 2] + edges[2, 0]
         col_scale = own_weight_slab / column_total

time: 228 us -> 219 us (0.961)
  blocking collectives: 37.8 us -> 31.7 us
    psum x2 -> x0, blocking collectives: 37.8 us -> none  [shards(): slab_parts = lax.psum(column_parts, 'narrow')]
    all_gather x0 -> x2, blocking collectives: none -> 31.7 us  [shards(): slab_parts = jnp.sum(lax.all_gather(column_parts, 'narrow'), axis=0)]
    reduce_scatter x1, waiting for transfers between devices: 61.8 us -> 56.9 us  [shards(): lax.psum_scatter(neighbours[0] + neighbours[2] + neighbours[4], 'narrow',...]
where the time goes in v1:
time: 219 us; the launch traced here: 218 us
  waiting for transfers between devices  119 us (54%)
  starting transfers between devices  34.4 us (16%)
  blocking collectives  31.7 us (14%)
  between operations  14.3 us (7%)
  other arithmetic  13.5 us (6%)
  matrix products  4.31 us (2%)
    ppermute x6, waiting for transfers between devices, extended(): lax.ppermute(lax.slice_in_dim(block, 0, width, axis=dim), axis, backward)  56.9 us
    reduce_scatter x1, waiting for transfers between devices, shards(): lax.psum_scatter(neighbours[0] + neighbours[2] + neighbours[4], 'narrow',...  56.9 us
    all_gather x2, blocking collectives, shards(): slab_parts = jnp.sum(lax.all_gather(column_parts, 'narrow'), axis=0)  31.7 us
    ppermute x6, starting transfers between devices, extended(): lax.ppermute(lax.slice_in_dim(block, block.shape[dim] - width, None, axis...  26.6 us
    ppermute x6, starting transfers between devices, extended(): lax.ppermute(lax.slice_in_dim(block, 0, width, axis=dim), axis, backward)  7.74 us
    ppermute x6, waiting for transfers between devices, extended(): lax.ppermute(lax.slice_in_dim(block, block.shape[dim] - width, None, axis...  4.93 us
  transfers between devices with their start and end apart: 13, of which 9 were waited for; matrix products, arithmetic and copies ran while one was open for 3% of the time, Pallas kernels for 0%

profile of v1, /device:TPU:1, one launch (start us, length us, event | category | flops | bytes accessed | tf_op | source)
XLA Modules:
  0.0 218.5 jit_solution(2672861399812301955)
XLA Ops:
  7.2 0.0 reduce-scatter.2.cloned.1.call-start
  7.2 1.5 fusion.2
  8.8 1.5 fusion.13
  10.3 1.3 collective-permute-start.1
  11.6 5.1 %collective-permute-start = (bf16[1,1024,512]{2,1,0:T(8,128)(2,1)S(1)}, bf16[1,1024,512]{2,1,0:T(8,128)(2,1)S(1)}, u32[]{:S(2)}, u32[]{:S(2)}) collective-permute-start(bf16[1,1024,512]{2,1,0:T(8,128)(2,1)S(1)} %fusion.13), channel_id=1, source_target_pairs={{0,4},{4,8},{8,12},{12,16},{16,20},{20,24},{24,28},{28,32},{32,36}... | collective-permute-start | bytes 3145736 | tf_op jit(solution)/shard_map/ppermute | solution.py:16
  16.7 0.1 fusion.5
  16.8 15.2 %collective-permute-done.1 = bf16[1,1024,512]{2,1,0:T(8,128)(2,1)S(1)} collective-permute-done((bf16[1,1024,512]{2,1,0:T(8,128)(2,1)S(1)}, bf16[1,1024,512]{2,1,0:T(8,128)(2,1)S(1)}, u32[]{:S(2)}, u32[]{:S(2)}) %collective-permute-start.1) | collective-permute-done | bytes 1048608 | tf_op jit(solution)/shard_map/ppermute | solution.py:19
  32.1 0.9 collective-permute-done
  33.0 0.3 pad_maximum_fusion
  33.3 0.3 broadcast_in_dim.16
  33.6 0.0 copy-start.3
  33.6 1.3 fusion.10
  35.0 0.0 copy-done
  35.0 0.4 multiply_reduce_fusion.1
  35.4 24.2 %all_gather.6 = f32[4,3,1024]{2,1,0:T(4,128)S(1)} all-gather(f32[1,3,1024]{2,1,0:T(4,128)S(1)} %all_gather_reshape.6), channel_id=1, replica_groups=mesh['wide'=128,'narrow'=4] {'narrow'}, dimensions={0}, use_global_device_ids=true | all-gather | bytes 61440 | tf_op jit(solution)/shard_map/all_gather | solution.py:62
  59.7 1.3 collective-permute-start.3
  61.0 4.0 %collective-permute-start.2 = (f32[1,3,1024]{2,1,0:T(4,128)S(1)}, f32[1,3,1024]{2,1,0:T(4,128)S(1)}, u32[]{:S(2)}, u32[]{:S(2)}) collective-permute-start(f32[1,3,1024]{2,1,0:T(4,128)S(1)} %bitcast.27), channel_id=1, source_target_pairs={{0,4},{4,8},{8,12},{12,16},{16,20},{20,24},{24,28},{28,32},{32,36}... | collective-permute-start | bytes 36872 | tf_op jit(solution)/shard_map/ppermute | solution.py:16
  65.0 0.0 collective-permute-done.3
  65.0 0.8 collective-permute-done.2
  65.8 0.7 dynamic-slice_divide_fusion.1
  66.5 1.3 collective-permute-start.5
  67.8 4.3 %collective-permute-start.4 = (f32[1,1024]{1,0:T(1,128)S(1)}, f32[1,1024]{1,0:T(1,128)S(1)}, u32[]{:S(2)}, u32[]{:S(2)}) collective-permute-start(f32[1,1024]{1,0:T(1,128)S(1)} %bitcast.36), channel_id=1, source_target_pairs={{0,4},{4,8},{8,12},{12,16},{16,20},{20,24},{24,28},{28,32},{32,36}... | collective-permute-start | bytes 12296 | tf_op jit(solution)/shard_map/ppermute | solution.py:16
  72.1 0.7 collective-permute-done.4
  72.9 0.3 multiply_reduce_fusion
  73.2 0.4 multiply_reduce_fusion.3
  73.6 7.5 %all_gather.7 = f32[4,3,1024]{2,1,0:T(4,128)S(1)} all-gather(f32[1,3,1024]{2,1,0:T(4,128)S(1)} %all_gather_reshape.7), channel_id=1, replica_groups=mesh['wide'=128,'narrow'=4] {'narrow'}, dimensions={0}, use_global_device_ids=true | all-gather | bytes 61440 | tf_op jit(solution)/shard_map/all_gather | solution.py:62
  81.2 1.3 collective-permute-start.7
  82.5 4.5 %collective-permute-start.6 = (f32[1,3,1024]{2,1,0:T(4,128)S(1)}, f32[1,3,1024]{2,1,0:T(4,128)S(1)}, u32[]{:S(2)}, u32[]{:S(2)}) collective-permute-start(f32[1,3,1024]{2,1,0:T(4,128)S(1)} %bitcast.30), channel_id=1, source_target_pairs={{0,4},{4,8},{8,12},{12,16},{16,20},{20,24},{24,28},{28,32},{32,36}... | collective-permute-start | bytes 36872 | tf_op jit(solution)/shard_map/ppermute | solution.py:16
  87.0 0.8 collective-permute-done.6
  87.9 0.7 dynamic-slice_divide_fusion
  88.6 1.3 collective-permute-start.9
  89.9 4.3 %collective-permute-start.8 = (f32[1,1024]{1,0:T(1,128)S(1)}, f32[1,1024]{1,0:T(1,128)S(1)}, u32[]{:S(2)}, u32[]{:S(2)}) collective-permute-start(f32[1,1024]{1,0:T(1,128)S(1)} %bitcast.33), channel_id=1, source_target_pairs={{0,4},{4,8},{8,12},{12,16},{16,20},{20,24},{24,28},{28,32},{32,36}... | collective-permute-start | bytes 12296 | tf_op jit(solution)/shard_map/ppermute | solution.py:16
  94.2 0.0 collective-permute-done.9
  94.2 0.7 collective-permute-done.8
  94.9 1.1 fusion.7
  96.1 0.4 slice_bitcast_fusion.1
  96.5 1.3 collective-permute-start.11
  97.8 4.5 %collective-permute-start.10 = (f32[1,1024,512]{2,1,0:T(8,128)S(1)}, f32[1,1024,512]{2,1,0:T(8,128)S(1)}, u32[]{:S(2)}, u32[]{:S(2)}) collective-permute-start(f32[1,1024,512]{2,1,0:T(8,128)S(1)} %get-tuple-element.2), channel_id=1, source_target_pairs={{0,4},{4,8},{8,12},{12,16},{16,20},{20,24},{24,28},{28,32},{32,36}... | collective-permute-start | bytes 6291464 | tf_op jit(solution)/shard_map/ppermute | solution.py:16
  102.3 41.6 %collective-permute-done.11 = f32[1,1024,512]{2,1,0:T(8,128)S(1)} collective-permute-done((f32[1,1024,512]{2,1,0:T(8,128)S(1)}, f32[1,1024,512]{2,1,0:T(8,128)S(1)}, u32[]{:S(2)}, u32[]{:S(2)}) %collective-permute-start.11) | collective-permute-done | bytes 2097184 | tf_op jit(solution)/shard_map/ppermute | solution.py:19
  143.9 0.9 collective-permute-done.10
  144.8 2.1 fusion.4
  147.0 0.0 reduce-scatter.2.cloned.1.call-update
  147.0 0.8 dynamic_slice.10
  147.8 2.7 %fusion.3 = bf16[1024,512]{1,0:T(8,128)(2,1)} fusion(bf16[1024,512]{1,0:T(8,128)(2,1)} %param.6, f32[1024]{0:T(1024)S(1)} %add_rsqrt_fusion), kind=kLoop, calls=%fused_computation.12 | loop fusion | flops 1572864 | bytes 2101248 | tf_op jit(solution)/shard_map/convert_element_type | solution.py:26
  150.4 0.5 multiply_reduce_fusion.2
  150.9 1.8 convolution_subtract_fusion
  152.7 56.9 %reduce-scatter.2.cloned.1.call-done = f32[256,512]{1,0:T(8,128)} async-done(((f32[1024,512]{1,0:T(8,128)}), f32[256,512]{1,0:T(8,128)}) %reduce-scatter.2.cloned.1.call-update) | async-done | bytes 524304 | tf_op jit(solution)/shard_map/reduce_scatter | solution.py:77
  209.6 2.0 multiply_subtract_fusion
  (25 shorter events, 0.2 us)
Async XLA Ops:
  7.2 9.5 %copy-start.2 = (bf16[256,512]{1,0:T(8,128)(2,1)S(1)}, bf16[256,512]{1,0:T(8,128)(2,1)}, u32[]{:S(2)}) copy-start(bf16[256,512]{1,0:T(8,128)(2,1)} %param.5) | copy-start | bytes 786436
  7.2 9.6 %copy-start.4 = (s32[2,24]{1,0:T(2,128)S(1)}, s32[2,24]{1,0:T(2,128)}, u32[]{:S(2)}) copy-start(s32[2,24]{1,0:T(2,128)} %param.9) | copy-start | bytes 580
  7.2 202.4 %reduce-scatter.2.cloned.1.call-start = ((), (), s32[]{:S(2)}) async-start(), calls=%async_computation.1 | async-start | bytes 2621440 | tf_op jit(solution)/shard_map/reduce_scatter | solution.py:77
  10.3 21.8 %collective-permute-start.1 = (bf16[1,1024,512]{2,1,0:T(8,128)(2,1)S(1)}, bf16[1,1024,512]{2,1,0:T(8,128)(2,1)S(1)}, u32[]{:S(2)}, u32[]{:S(2)}) collective-permute-start(bf16[1,1024,512]{2,1,0:T(8,128)(2,1)S(1)} %fusion.13), channel_id=1, source_target_pairs={{4,0},{8,4},{12,8},{16,12},{20,16},{24,20},{28,24},{32,28},{36,32}... | collective-permute-start | bytes 3145736 | tf_op jit(solution)/shard_map/ppermute | solution.py:19
  11.6 21.4 %collective-permute-start = (bf16[1,1024,512]{2,1,0:T(8,128)(2,1)S(1)}, bf16[1,1024,512]{2,1,0:T(8,128)(2,1)S(1)}, u32[]{:S(2)}, u32[]{:S(2)}) collective-permute-start(bf16[1,1024,512]{2,1,0:T(8,128)(2,1)S(1)} %fusion.13), channel_id=1, source_target_pairs={{0,4},{4,8},{8,12},{12,16},{16,20},{20,24},{24,28},{28,32},{32,36}... | collective-permute-start | bytes 3145736 | tf_op jit(solution)/shard_map/ppermute | solution.py:16
  33.3 1.7 copy-start
  33.6 1.4 copy-start.3
  59.7 5.3 %collective-permute-start.3 = (f32[1,3,1024]{2,1,0:T(4,128)S(1)}, f32[1,3,1024]{2,1,0:T(4,128)S(1)}, u32[]{:S(2)}, u32[]{:S(2)}) collective-permute-start(f32[1,3,1024]{2,1,0:T(4,128)S(1)} %bitcast.26), channel_id=1, source_target_pairs={{4,0},{8,4},{12,8},{16,12},{20,16},{24,20},{28,24},{32,28},{36,32}... | collective-permute-start | bytes 36872 | tf_op jit(solution)/shard_map/ppermute | solution.py:19
  61.0 4.8 %collective-permute-start.2 = (f32[1,3,1024]{2,1,0:T(4,128)S(1)}, f32[1,3,1024]{2,1,0:T(4,128)S(1)}, u32[]{:S(2)}, u32[]{:S(2)}) collective-permute-start(f32[1,3,1024]{2,1,0:T(4,128)S(1)} %bitcast.27), channel_id=1, source_target_pairs={{0,4},{4,8},{8,12},{12,16},{16,20},{20,24},{24,28},{28,32},{32,36}... | collective-permute-start | bytes 36872 | tf_op jit(solution)/shard_map/ppermute | solution.py:16
  66.5 5.6 %collective-permute-start.5 = (f32[1,1024]{1,0:T(1,128)S(1)}, f32[1,1024]{1,0:T(1,128)S(1)}, u32[]{:S(2)}, u32[]{:S(2)}) collective-permute-start(f32[1,1024]{1,0:T(1,128)S(1)} %bitcast.35), channel_id=1, source_target_pairs={{4,0},{8,4},{12,8},{16,12},{20,16},{24,20},{28,24},{32,28},{36,32}... | collective-permute-start | bytes 12296 | tf_op jit(solution)/shard_map/ppermute | solution.py:19
  67.8 5.0 %collective-permute-start.4 = (f32[1,1024]{1,0:T(1,128)S(1)}, f32[1,1024]{1,0:T(1,128)S(1)}, u32[]{:S(2)}, u32[]{:S(2)}) collective-permute-start(f32[1,1024]{1,0:T(1,128)S(1)} %bitcast.36), channel_id=1, source_target_pairs={{0,4},{4,8},{8,12},{12,16},{16,20},{20,24},{24,28},{28,32},{32,36}... | collective-permute-start | bytes 12296 | tf_op jit(solution)/shard_map/ppermute | solution.py:16
  81.2 5.8 %collective-permute-start.7 = (f32[1,3,1024]{2,1,0:T(4,128)S(1)}, f32[1,3,1024]{2,1,0:T(4,128)S(1)}, u32[]{:S(2)}, u32[]{:S(2)}) collective-permute-start(f32[1,3,1024]{2,1,0:T(4,128)S(1)} %bitcast.29), channel_id=1, source_target_pairs={{4,0},{8,4},{12,8},{16,12},{20,16},{24,20},{28,24},{32,28},{36,32}... | collective-permute-start | bytes 36872 | tf_op jit(solution)/shard_map/ppermute | solution.py:19
  82.5 5.4 %collective-permute-start.6 = (f32[1,3,1024]{2,1,0:T(4,128)S(1)}, f32[1,3,1024]{2,1,0:T(4,128)S(1)}, u32[]{:S(2)}, u32[]{:S(2)}) collective-permute-start(f32[1,3,1024]{2,1,0:T(4,128)S(1)} %bitcast.30), channel_id=1, source_target_pairs={{0,4},{4,8},{8,12},{12,16},{16,20},{20,24},{24,28},{28,32},{32,36}... | collective-permute-start | bytes 36872 | tf_op jit(solution)/shard_map/ppermute | solution.py:16
  88.6 5.6 %collective-permute-start.9 = (f32[1,1024]{1,0:T(1,128)S(1)}, f32[1,1024]{1,0:T(1,128)S(1)}, u32[]{:S(2)}, u32[]{:S(2)}) collective-permute-start(f32[1,1024]{1,0:T(1,128)S(1)} %bitcast.32), channel_id=1, source_target_pairs={{4,0},{8,4},{12,8},{16,12},{20,16},{24,20},{28,24},{32,28},{36,32}... | collective-permute-start | bytes 12296 | tf_op jit(solution)/shard_map/ppermute | solution.py:19
  89.9 5.0 %collective-permute-start.8 = (f32[1,1024]{1,0:T(1,128)S(1)}, f32[1,1024]{1,0:T(1,128)S(1)}, u32[]{:S(2)}, u32[]{:S(2)}) collective-permute-start(f32[1,1024]{1,0:T(1,128)S(1)} %bitcast.33), channel_id=1, source_target_pairs={{0,4},{4,8},{8,12},{12,16},{16,20},{20,24},{24,28},{28,32},{32,36}... | collective-permute-start | bytes 12296 | tf_op jit(solution)/shard_map/ppermute | solution.py:16
  96.5 47.4 %collective-permute-start.11 = (f32[1,1024,512]{2,1,0:T(8,128)S(1)}, f32[1,1024,512]{2,1,0:T(8,128)S(1)}, u32[]{:S(2)}, u32[]{:S(2)}) collective-permute-start(f32[1,1024,512]{2,1,0:T(8,128)S(1)} %get-tuple-element.3), channel_id=1, source_target_pairs={{4,0},{8,4},{12,8},{16,12},{20,16},{24,20},{28,24},{32,28},{36,32}... | collective-permute-start | bytes 6291464 | tf_op jit(solution)/shard_map/ppermute | solution.py:19
  97.8 47.0 %collective-permute-start.10 = (f32[1,1024,512]{2,1,0:T(8,128)S(1)}, f32[1,1024,512]{2,1,0:T(8,128)S(1)}, u32[]{:S(2)}, u32[]{:S(2)}) collective-permute-start(f32[1,1024,512]{2,1,0:T(8,128)S(1)} %get-tuple-element.2), channel_id=1, source_target_pairs={{0,4},{4,8},{8,12},{12,16},{16,20},{20,24},{24,28},{28,32},{32,36}... | collective-permute-start | bytes 6291464 | tf_op jit(solution)/shard_map/ppermute | solution.py:16
  147.8 3.2 %copy-start.1 = (bf16[3,1024,512]{2,1,0:T(8,128)(2,1)S(1)}, bf16[3,1024,512]{2,1,0:T(8,128)(2,1)}, u32[]{:S(2)}) copy-start(bf16[3,1024,512]{2,1,0:T(8,128)(2,1)} %copy-done) | copy-start | bytes 9437188
Sparse Core Ops, SparseCore 0:
  147.1 62.4 reduce-scatter.1
